TPU v7x, 256 devices: a whole 4x4x8 slice. The times are simulated.
256 devices in a mesh: dp: 2 (over y_hi), fsdp: 16 (over x, y_lo, core), tensor: 8 (over z).
Axes of the slice: x: 4, y: 4 (y_hi: 2, y_lo: 2; y = y_hi * 2 + y_lo), z: 8, core: 2. Of those that a mesh axis runs over, the one named last changes fastest.
Arguments:
- activations: bfloat16 [4096, 8192], P(('dp', 'fsdp'), 'tensor'), may hold values from -6 to 6
- cotangent: bfloat16 [4096, 8192], P(('dp', 'fsdp'), 'tensor'), may hold values from -6 to 6
- up_tiles: bfloat16 [1024, 128, 128], P(('fsdp', 'tensor')), may hold values from -0.1875 to 0.1875
- down_tiles: bfloat16 [1024, 128, 128], P(('fsdp', 'tensor')), may hold values from -0.125 to 0.125
- up_rows: int32 [128, 8], P(None, 'tensor'), may hold values from 0 to 63, as said below
- up_cols: int32 [128, 8], P(None, 'tensor'), may hold values from 0 to 15, as said below
- down_rows: int32 [128, 8], P(None, 'tensor'), may hold values from 0 to 15, as said below
- down_cols: int32 [128, 8], P(None, 'tensor'), may hold values from 0 to 63, as said below
Outputs:
- output: bfloat16 [4096, 8192], P(('dp', 'fsdp'), 'tensor')
- input_grad: bfloat16 [4096, 8192], P(('dp', 'fsdp'), 'tensor')
- up_grad: float32 [1024, 128, 128], P(('fsdp', 'tensor'))
- down_grad: float32 [1024, 128, 128], P(('fsdp', 'tensor'))
Inputs may be any that keep to these rules, and one draw needn't show every extreme that they name: `up_rows`: within a column, the up tiles of one hidden-unit block name distinct feature blocks. `up_cols`: every value occurs exactly 8 times in each column. `down_rows`: every value occurs exactly 8 times in each column. `down_cols`: within a column, the down tiles of one hidden-unit block name distinct feature blocks.
All inputs are finite; a program needn't handle non-finite values.
Results may differ from a plain program's by a relative error of at most 0.018.
Values may be sent and summed in bfloat16 or wider, within the bound.
No kernel may reach another device: no remote copies, remote signals or barrier semaphores. Data moves between devices by JAX's collectives and lax.ppermute only.
A program may use at most 128 MiB of HBM per device.

v0:
```python
import jax
import jax.numpy as jnp
from jax import lax
from jax.sharding import PartitionSpec as P

D = 8192
FF = 16384
inv_root_two = 0.7071067811865476
inv_root_tau = 0.3989422804014327


def gelu_parts(values):
    normal_cdf = 0.5 * (1.0 + jax.scipy.special.erf(values * inv_root_two))
    density = inv_root_tau * jnp.exp(-0.5 * values * values)
    return (values * normal_cdf, normal_cdf + values * density)


def grouped_pick(acting, far_index, hidden_blocks, block_size):
    rows_here = acting.shape[0]
    picked = acting.reshape(rows_here, -1, block_size)[:, far_index]
    return picked.reshape(rows_here, hidden_blocks, -1, block_size)


def add_far(product, far_index, model_blocks):
    rows_here = product.shape[0]
    block_size = product.shape[-1]
    flat = product.reshape(rows_here, -1, block_size)
    summed = (
        jnp.zeros((rows_here, model_blocks, block_size), jnp.float32).at[:, far_index].add(flat)
    )
    return summed.reshape(rows_here, model_blocks * block_size)


def grouped_tiles(tiles, order, hidden_blocks):
    block_size = tiles.shape[1]
    return tiles[order].reshape(hidden_blocks, -1, block_size, block_size)


def body(activations, cotangent, up_tiles, down_tiles, up_rows, up_cols, down_rows, down_cols):
    block_size = up_tiles.shape[1]
    hidden_blocks = FF // (block_size * lax.axis_size("tensor"))
    model_blocks = D // block_size
    up_order = jnp.argsort(up_cols[:, 0], stable=True)
    down_order = jnp.argsort(down_rows[:, 0], stable=True)
    up_back = jnp.argsort(up_order)
    down_back = jnp.argsort(down_order)
    up_far = up_rows[:, 0][up_order]
    down_far = down_cols[:, 0][down_order]
    full_input = lax.all_gather(activations, "tensor", axis=1, tiled=True)
    input_pick = grouped_pick(full_input, up_far, hidden_blocks, block_size)
    up_whole = lax.all_gather(up_tiles, "fsdp", axis=0, tiled=True)
    up_sorted = grouped_tiles(up_whole, up_order, hidden_blocks)
    pre_act = jnp.einsum(
        "thkb,hkbc->thc", input_pick, up_sorted, preferred_element_type=jnp.float32
    )
    gelu_out, gelu_slope = gelu_parts(pre_act)
    hidden = gelu_out.astype(jnp.bfloat16)
    down_whole = lax.all_gather(down_tiles, "fsdp", axis=0, tiled=True)
    down_sorted = grouped_tiles(down_whole, down_order, hidden_blocks)
    out_product = jnp.einsum(
        "thb,hkbc->thkc", hidden, down_sorted, preferred_element_type=jnp.float32
    )
    partial_out = add_far(out_product, down_far, model_blocks)
    output = lax.psum_scatter(
        partial_out.astype(jnp.bfloat16), "tensor", scatter_dimension=1, tiled=True
    )
    full_cotangent = lax.all_gather(cotangent, "tensor", axis=1, tiled=True)
    cot_pick = grouped_pick(full_cotangent, down_far, hidden_blocks, block_size)
    hidden_grad = jnp.einsum(
        "thkc,hkbc->thb", cot_pick, down_sorted, preferred_element_type=jnp.float32
    )
    pre_grad = (hidden_grad * gelu_slope).astype(jnp.bfloat16)
    in_product = jnp.einsum(
        "thc,hkbc->thkb", pre_grad, up_sorted, preferred_element_type=jnp.float32
    )
    partial_in = add_far(in_product, up_far, model_blocks)
    input_grad = lax.psum_scatter(
        partial_in.astype(jnp.bfloat16), "tensor", scatter_dimension=1, tiled=True
    )
    up_grouped = jnp.einsum(
        "thkb,thc->hkbc", input_pick, pre_grad, preferred_element_type=jnp.float32
    )
    down_grouped = jnp.einsum(
        "thb,thkc->hkbc", hidden, cot_pick, preferred_element_type=jnp.float32
    )
    up_rounded = up_grouped.astype(jnp.bfloat16).reshape(-1, block_size, block_size)
    down_rounded = down_grouped.astype(jnp.bfloat16).reshape(-1, block_size, block_size)
    up_term = up_rounded[up_back].astype(jnp.float32)
    down_term = down_rounded[down_back].astype(jnp.float32)
    up_part, down_part = (
        lax.psum_scatter(
            up_term.astype(jnp.bfloat16), "fsdp", scatter_dimension=0, tiled=True
        ).astype(jnp.float32),
        lax.psum_scatter(
            down_term.astype(jnp.bfloat16), "fsdp", scatter_dimension=0, tiled=True
        ).astype(jnp.float32),
    )
    up_grad, down_grad = (
        lax.psum(up_part.astype(jnp.bfloat16), "dp").astype(jnp.float32),
        lax.psum(down_part.astype(jnp.bfloat16), "dp").astype(jnp.float32),
    )
    return (output, input_grad, up_grad, down_grad)


def solution(mesh):
    in_specs = (
        P(("dp", "fsdp"), "tensor"),
        P(("dp", "fsdp"), "tensor"),
        P(("fsdp", "tensor"), None, None),
        P(("fsdp", "tensor"), None, None),
        P(None, "tensor"),
        P(None, "tensor"),
        P(None, "tensor"),
        P(None, "tensor"),
    )
    out_specs = (
        P(("dp", "fsdp"), "tensor"),
        P(("dp", "fsdp"), "tensor"),
        P(("fsdp", "tensor"), None, None),
        P(("fsdp", "tensor"), None, None),
    )
    return jax.shard_map(body, mesh=mesh, in_specs=in_specs, out_specs=out_specs, check_vma=False)
```

profile of v0, /device:TPU:1, one launch (start us, length us, event | category | flops | bytes accessed | tf_op | source)
XLA Modules:
  0.0 480.6 jit_solution(9236470539080875752)
XLA Ops:
  7.2 1.8 copy.58
  9.1 1.8 copy.65
  11.0 0.7 all-gather.7.cloned.1.call-update
  11.7 0.5 all-gather.5.cloned.1.call-update
  12.3 3.2 sort.63
  15.5 2.5 sort.64
  18.0 1.2 gather_fusion.3
  19.3 3.2 sort.62
  22.5 1.6 gather_fusion
  24.1 28.0 %all-gather.9.cloned.1.call-done = bf16[128,8192]{0,1:T(8,128)(2,1)} async-done(((bf16[128,1024]{0,1:T(8,128)(2,1)}), bf16[128,8192]{0,1:T(8,128)(2,1)}) %all-gather.9.cloned.1.call-update) | async-done | bytes 2097168 | tf_op jit(solution)/shard_map/all_gather | solution.py:49
  52.1 3.2 copy.59
  55.3 39.0 %all-gather.11.cloned.1.call-done = bf16[128,8192]{0,1:T(8,128)(2,1)} async-done(((bf16[128,1024]{0,1:T(8,128)(2,1)}), bf16[128,8192]{0,1:T(8,128)(2,1)}) %all-gather.11.cloned.1.call-update) | async-done | bytes 2097168 | tf_op jit(solution)/shard_map/all_gather | solution.py:67
  94.3 4.1 copy.66
  98.4 3.0 gather_fusion.4
  101.4 4.6 gather_fusion.5
  106.0 32.7 %all-gather.7.cloned.1.call-done = bf16[128,128,128]{2,1,0:T(8,128)(2,1)} async-done(((bf16[8,128,128]{2,1,0:T(8,128)(2,1)}), bf16[128,128,128]{2,1,0:T(8,128)(2,1)}) %all-gather.7.cloned.1.call-update) | async-done | bytes 4194320 | tf_op jit(solution)/shard_map/all_gather | solution.py:51
  138.7 5.2 %gather_fusion.2 = bf16[128,128,128]{2,1,0:T(8,128)(2,1)} fusion(bf16[128,128,128]{2,1,0:T(8,128)(2,1)} %all-gather.7.cloned.1.call-done, s32[1024]{0:T(1024)S(1)} %pad_clamp_fusion.4), kind=kCustom, calls=%fused_computation.2 | custom fusion | bytes 8389120 | tf_op jit(solution)/shard_map/gather | solution.py:36
  143.9 4.8 convolution_bitcast_fusion.1
  148.7 31.7 %all-gather.5.cloned.1.call-done = bf16[128,128,128]{2,1,0:T(8,128)(2,1)} async-done(((bf16[8,128,128]{2,1,0:T(8,128)(2,1)}), bf16[128,128,128]{2,1,0:T(8,128)(2,1)}) %all-gather.5.cloned.1.call-update) | async-done | bytes 4194320 | tf_op jit(solution)/shard_map/all_gather | solution.py:58
  180.5 5.2 %gather_fusion.1 = bf16[128,128,128]{2,1,0:T(8,128)(2,1)} fusion(bf16[128,128,128]{2,1,0:T(8,128)(2,1)} %all-gather.5.cloned.1.call-done, s32[1024]{0:T(1024)S(1)} %pad_clamp_fusion.5), kind=kCustom, calls=%fused_computation.1 | custom fusion | bytes 8389120 | tf_op jit(solution)/shard_map/gather | solution.py:36
  185.7 5.0 %fusion.2 = bf16[128,16,128,1]{0,2,3,1:T(8,128)(2,1)S(1)} fusion(bf16[16,8,128,128]{3,2,1,0:T(8,128)(2,1)} %bitcast.84, bf16[128,16,8,128]{3,0,2,1:T(8,128)(2,1)} %bitcast.86, f32[128,16,128]{0,2,1:T(8,128)S(1)} %convolution_bitcast_fusion.1), kind=kOutput, calls=%fused_computation.17 | convolution fusion | flops 539492352 | bytes 9961472 | tf_op jit(solution)/shard_map/thkc,hkbc->thb/dot_general | solution.py:69
  190.7 3.3 convolution_convert_fusion.1
  194.0 5.2 %gather_fusion.6 = bf16[128,128,128]{2,1,0:T(8,128)(2,1)} fusion(bf16[128,128,128]{2,1,0:T(8,128)(2,1)} %bitcast.88, s32[1024]{0:T(1024)S(1)} %pad_clamp_fusion.1), kind=kCustom, calls=%fused_computation.6 | custom fusion | bytes 8389120 | tf_op jit(solution)/shard_map/gather | solution.py:88
  199.2 0.2 reduce-scatter.11.cloned.1.call-start
  199.5 2.5 sort.65
  202.0 5.6 %convolution_convert_fusion = bf16[16,8,128,128]{3,2,1,0:T(8,128)(2,1)} fusion(bf16[128,16,8,128]{3,0,2,1:T(8,128)(2,1)} %bitcast.87, f32[128,16,128]{0,2,1:T(8,128)S(1)} %convolution_bitcast_fusion.1), kind=kOutput, calls=%fused_computation.10 | convolution fusion | flops 540278784 | bytes 9437184 | tf_op jit(solution)/shard_map/thb,thkc->hkbc/dot_general | solution.py:83
  207.6 6.4 %copy.74 = bf16[128,128,128]{2,1,0:T(8,128)(2,1)} copy(bf16[128,128,128]{1,2,0:T(8,128)(2,1)} %bitcast.89) | data formatting | bytes 8388608 | tf_op jit(solution)/shard_map/reshape | solution.py:87
  214.0 5.3 %gather_fusion.7 = bf16[128,128,128]{2,1,0:T(8,128)(2,1)} fusion(bf16[128,128,128]{2,1,0:T(8,128)(2,1)} %copy.74, s32[1024]{0:T(1024)S(1)} %pad_clamp_fusion), kind=kCustom, calls=%fused_computation.7 | custom fusion | bytes 8389120 | tf_op jit(solution)/shard_map/gather | solution.py:89
  219.4 6.7 %fusion.13 = f32[16,8,128,128]{3,2,1,0:T(8,128)} fusion(bf16[16,8,128,128]{3,2,1,0:T(8,128)(2,1)} %bitcast.77, bf16[128,16,128,1]{0,2,3,1:T(8,128)(2,1)S(1)} %fusion.2), kind=kOutput, calls=%fused_computation.40 | convolution fusion | flops 536870912 | bytes 13107200 | tf_op jit(solution)/shard_map/thc,hkbc->thkb/dot_general | solution.py:73
  226.1 9.0 %copy.68 = f32[128,128,128]{2,0,1:T(8,128)} copy(f32[128,128,128]{0,2,1:T(8,128)} %bitcast.82) | data formatting | bytes 16777216 | tf_op jit(solution)/shard_map/reshape | solution.py:27
  235.1 2.5 broadcast.42.clone.1
  237.6 26.7 %scatter_fusion.1 = f32[128,64,128]{2,0,1:T(8,128)} fusion(f32[128,64,128]{2,0,1:T(8,128)} %broadcast.42.clone.1, s32[128]{0:T(128)S(1)} %fusion.9, f32[128,128,128]{2,1,0:T(8,128)} %bitcast.81), kind=kCustom, calls=%fused_computation.9 | custom fusion | flops 2097152 | bytes 25166336 | tf_op jit(solution)/shard_map/scatter-add | solution.py:29
  264.3 2.6 convert_element_type.45
  266.9 2.9 copy.69
  270.0 6.8 %fusion.11 = f32[16,8,128,128]{3,2,1,0:T(8,128)} fusion(bf16[16,8,128,128]{3,2,1,0:T(8,128)(2,1)} %bitcast.85, f32[128,16,128]{0,2,1:T(8,128)S(1)} %convolution_bitcast_fusion.1), kind=kOutput, calls=%fused_computation.39 | convolution fusion | flops 538181632 | bytes 13631488 | tf_op jit(solution)/shard_map/thb,hkbc->thkc/dot_general | solution.py:60
  276.7 9.0 %copy.63 = f32[128,128,128]{2,0,1:T(8,128)} copy(f32[128,128,128]{0,2,1:T(8,128)} %bitcast.83) | data formatting | bytes 16777216 | tf_op jit(solution)/shard_map/reshape | solution.py:27
  285.8 2.5 broadcast.42.clone
  288.2 26.9 %scatter_fusion = f32[128,64,128]{2,0,1:T(8,128)} fusion(f32[128,64,128]{2,0,1:T(8,128)} %broadcast.42.clone, s32[128]{0:T(128)S(1)} %fusion.8, f32[128,128,128]{2,1,0:T(8,128)} %bitcast.80), kind=kCustom, calls=%fused_computation.8 | custom fusion | flops 2097152 | bytes 25166336 | tf_op jit(solution)/shard_map/scatter-add | solution.py:29
  315.1 2.6 convert_element_type.42
  317.7 2.9 copy.64
  320.7 16.4 %reduce-scatter.11.cloned.1.call-done = bf16[8,128,128]{2,1,0:T(8,128)(2,1)} async-done(((bf16[128,128,128]{2,1,0:T(8,128)(2,1)}), bf16[8,128,128]{2,1,0:T(8,128)(2,1)}) %reduce-scatter.11.cloned.1.call-update) | async-done | bytes 262160 | tf_op jit(solution)/shard_map/reduce_scatter | solution.py:94
  337.1 42.2 %reduce-scatter.7.cloned.1.call-done = bf16[128,1024]{0,1:T(8,128)(2,1)} async-done(((bf16[128,8192]{0,1:T(8,128)(2,1)}), bf16[128,1024]{0,1:T(8,128)(2,1)}) %reduce-scatter.7.cloned.1.call-update) | async-done | bytes 262160 | tf_op jit(solution)/shard_map/reduce_scatter | solution.py:77
  379.4 1.8 copy.76
  381.1 41.9 %reduce-scatter.5.cloned.1.call-done = bf16[128,1024]{0,1:T(8,128)(2,1)} async-done(((bf16[128,8192]{0,1:T(8,128)(2,1)}), bf16[128,1024]{0,1:T(8,128)(2,1)}) %reduce-scatter.5.cloned.1.call-update) | async-done | bytes 262160 | tf_op jit(solution)/shard_map/reduce_scatter | solution.py:64
  423.0 1.8 copy.75
  424.8 45.7 %all-reduce.3.cloned.1.call-done = (bf16[8,128,128]{2,1,0:T(8,128)(2,1)}, bf16[8,128,128]{2,1,0:T(8,128)(2,1)}) async-done(((bf16[8,128,128]{2,1,0:T(8,128)(2,1)}, bf16[8,128,128]{2,1,0:T(8,128)(2,1)}), (bf16[8,128,128]{2,1,0:T(8,128)(2,1)}, bf16[8,128,128]{2,1,0:T(8,128)(2,1)})) %all-reduce.3.cloned.1.call-update) | async-done | bytes 524304 | tf_op jit(solution)/shard_map/psum | solution.py:99
  470.5 1.8 convert_element_type.48
  472.3 1.8 convert_element_type.51
  (38 shorter events, 0.5 us)
Async XLA Ops:
  7.2 10.9 %copy-start = (s32[128,1]{0,1:T(1,128)S(1)}, s32[128,1]{0,1:T(1,128)}, u32[]{:S(2)}) copy-start(s32[128,1]{0,1:T(1,128)} %param.12) | copy-start | bytes 1540
  7.2 44.9 %all-gather.9.cloned.1.call-start = ((), (), s32[]{:S(2)}) async-start(), calls=%async_computation.6 | async-start | bytes 2359296 | tf_op jit(solution)/shard_map/all_gather | solution.py:49
  9.0 85.3 %all-gather.11.cloned.1.call-start = ((), (), s32[]{:S(2)}) async-start(), calls=%async_computation.8 | async-start | bytes 2359296 | tf_op jit(solution)/shard_map/all_gather | solution.py:67
  10.9 127.8 %all-gather.7.cloned.1.call-start = ((), (), s32[]{:S(2)}) async-start(), calls=%async_computation.5 | async-start | bytes 4456448 | tf_op jit(solution)/shard_map/all_gather | solution.py:51
  11.7 168.8 %all-gather.5.cloned.1.call-start = ((), (), s32[]{:S(2)}) async-start(), calls=%async_computation.4 | async-start | bytes 4456448 | tf_op jit(solution)/shard_map/all_gather | solution.py:58
  12.2 308.5 %reduce-scatter.9.cloned.1.call-start = ((), (), s32[]{:S(2)}) async-start(), calls=%async_computation.10 | async-start | bytes 4456448 | tf_op jit(solution)/shard_map/reduce_scatter | solution.py:91
  185.7 5.0 %copy-start.2 = (bf16[128,128,128]{2,1,0:T(8,128)(2,1)S(1)}, bf16[128,128,128]{2,1,0:T(8,128)(2,1)}, u32[]{:S(2)}) copy-start(bf16[128,128,128]{2,1,0:T(8,128)(2,1)} %gather_fusion.4) | copy-start | bytes 12582916
  199.2 137.9 %reduce-scatter.11.cloned.1.call-start = ((), (), s32[]{:S(2)}) async-start(), calls=%async_computation.11 | async-start | bytes 4456448 | tf_op jit(solution)/shard_map/reduce_scatter | solution.py:94
  219.4 160.0 %reduce-scatter.7.cloned.1.call-start = ((), (), s32[]{:S(2)}) async-start(), calls=%async_computation.9 | async-start | bytes 2359296 | tf_op jit(solution)/shard_map/reduce_scatter | solution.py:77
  269.9 153.1 %reduce-scatter.5.cloned.1.call-start = ((), (), s32[]{:S(2)}) async-start(), calls=%async_computation.7 | async-start | bytes 2359296 | tf_op jit(solution)/shard_map/reduce_scatter | solution.py:64
  315.1 158.9 %copy-start.1 = (s32[128,1]{0,1:T(1,128)S(1)}, s32[128,1]{0,1:T(1,128)}, u32[]{:S(2)}) copy-start(s32[128,1]{0,1:T(1,128)} %param.12) | copy-start | bytes 1540
  320.7 149.9 %all-reduce.3.cloned.1.call-start = ((), (), s32[]{:S(2)}) async-start(), calls=%async_computation.12 | async-start | bytes 1048576 | tf_op jit(solution)/shard_map/psum | solution.py:99
Sparse Core Ops, SparseCore 0:
  10.4 41.6 all-gather.8
  54.5 39.8 all-gather.10
  96.2 42.5 all-gather.6
  140.4 39.9 all-gather.4
  199.3 66.5 reduce-scatter.8
  268.4 68.6 reduce-scatter.10
  339.7 39.6 reduce-scatter.6
  381.9 41.0 reduce-scatter.4
  425.7 44.8 all-reduce.2
where the time goes:
time: 482 us; the launch traced here: 481 us
  waiting for transfers between devices  279 us (58%)
  local copies, waits for them, and re-layouts  81.1 us (17%)
  other arithmetic  73.8 us (15%)
  matrix products  32.2 us (7%)
  between operations  14 us (3%)
    scatter-add x2, other arithmetic, add_far(): jnp.zeros((rows_here, model_blocks, block_size), jnp.float32)  53.6 us
    psum x1, waiting for transfers between devices, body(): lax.psum(up_part.astype(jnp.bfloat16), 'dp').astype(jnp.float32)  45.7 us
    reduce_scatter x1, waiting for transfers between devices, body(): lax.psum_scatter(partial_in.astype(jnp.bfloat16), 'tensor', scatter_dimen...  42.2 us
    reduce_scatter x1, waiting for transfers between devices, body(): lax.psum_scatter(partial_out.astype(jnp.bfloat16), 'tensor', scatter_dime...  41.9 us
    all_gather x1, waiting for transfers between devices, body(): full_cotangent = lax.all_gather(cotangent, 'tensor', axis=1, tiled=True)  39 us
    all_gather x1, waiting for transfers between devices, body(): up_whole = lax.all_gather(up_tiles, 'fsdp', axis=0, tiled=True)  32.7 us
    all_gather x1, waiting for transfers between devices, body(): down_whole = lax.all_gather(down_tiles, 'fsdp', axis=0, tiled=True)  31.7 us
    all_gather x1, waiting for transfers between devices, body(): full_input = lax.all_gather(activations, 'tensor', axis=1, tiled=True)  28 us
  transfers between devices with their start and end apart: 9, of which 8 were waited for; matrix products, arithmetic and copies ran while one was open for 34% of the time, Pallas kernels for 0%

commit v1 on v0

--- a/solution.py
+++ b/solution.py
@@ -55,7 +55,9 @@
     )
     gelu_out, gelu_slope = gelu_parts(pre_act)
     hidden = gelu_out.astype(jnp.bfloat16)
-    down_whole = lax.all_gather(down_tiles, "fsdp", axis=0, tiled=True)
+    down_whole = jnp.concatenate(
+        lax.all_to_all(jnp.stack([down_tiles] * lax.axis_size("fsdp")), "fsdp", 0, 0), 0
+    )
     down_sorted = grouped_tiles(down_whole, down_order, hidden_blocks)
     out_product = jnp.einsum(
         "thb,hkbc->thkc", hidden, down_sorted, preferred_element_type=jnp.float32

time: 482 us -> 445 us (0.923)
  waiting for transfers between devices: 279 us -> 233 us
  starting transfers between devices: 0.55 us -> 8.14 us
  local copies, waits for them, and re-layouts: 81.1 us -> 86.5 us
    all_gather x1 -> x0, waiting for transfers between devices: 31.7 us -> none  [body(): down_whole = lax.all_gather(down_tiles, 'fsdp', axis=0, tiled=True)]
    all_gather x1, waiting for transfers between devices: 28 us -> 20 us  [body(): full_input = lax.all_gather(activations, 'tensor', axis=1, tiled=True)]
    all_to_all x0 -> x1, starting transfers between devices: none -> 7.63 us  [body(): lax.all_to_all(jnp.stack([down_tiles] * lax.axis_size('fsdp')), 'fsdp', 0...]
    all_gather x1, waiting for transfers between devices: 32.7 us -> 27.4 us  [body(): up_whole = lax.all_gather(up_tiles, 'fsdp', axis=0, tiled=True)]
  transfers between devices with their start and end apart: 9 -> 9, of which waited for: 8 -> 7; matrix products, arithmetic and copies ran while one was open for 34% -> 36% of each run, Pallas kernels for 0% -> 0%
where the time goes in v1:
time: 445 us; the launch traced here: 443 us
  waiting for transfers between devices  233 us (52%)
  local copies, waits for them, and re-layouts  86.5 us (19%)
  other arithmetic  72.5 us (16%)
  matrix products  28.7 us (6%)
  between operations  14.3 us (3%)
  starting transfers between devices  8.14 us (2%)
    scatter-add x2, other arithmetic, add_far(): jnp.zeros((rows_here, model_blocks, block_size), jnp.float32)  53.6 us
    psum x1, waiting for transfers between devices, body(): lax.psum(up_part.astype(jnp.bfloat16), 'dp').astype(jnp.float32)  46 us
    reduce_scatter x1, waiting for transfers between devices, body(): lax.psum_scatter(partial_in.astype(jnp.bfloat16), 'tensor', scatter_dimen...  42.2 us
    reduce_scatter x1, waiting for transfers between devices, body(): lax.psum_scatter(partial_out.astype(jnp.bfloat16), 'tensor', scatter_dime...  41.7 us
    all_gather x1, waiting for transfers between devices, body(): full_cotangent = lax.all_gather(cotangent, 'tensor', axis=1, tiled=True)  38.2 us
    all_gather x1, waiting for transfers between devices, body(): up_whole = lax.all_gather(up_tiles, 'fsdp', axis=0, tiled=True)  27.4 us
    all_gather x1, waiting for transfers between devices, body(): full_input = lax.all_gather(activations, 'tensor', axis=1, tiled=True)  20 us
    reshape x2, local copies, waits for them, and re-layouts, add_far(): flat = product.reshape(rows_here, -1, block_size)  18 us
  transfers between devices with their start and end apart: 9, of which 7 were waited for; matrix products, arithmetic and copies ran while one was open for 36% of the time, Pallas kernels for 0%

profile of v1, /device:TPU:1, one launch (start us, length us, event | category | flops | bytes accessed | tf_op | source)
XLA Modules:
  0.0 443.0 jit_solution(12582740605940836150)
XLA Ops:
  7.2 1.8 copy.58
  9.1 1.8 copy.65
  11.7 4.0 stack.2
  15.6 7.6 %all-to-all-start = ((bf16[16,8,128,128]{3,2,1,0:T(8,128)(2,1)}), bf16[16,8,128,128]{3,2,1,0:T(8,128)(2,1)}, u32[]{:S(2)}, u32[]{:S(2)}) async-start(bf16[16,8,128,128]{3,2,1,0:T(8,128)(2,1)} %stack.2), calls=%async_computation | async-start | bytes 8388608 | tf_op jit(solution)/shard_map/all_to_all | solution.py:59
  23.3 2.5 sort.63
  25.9 2.5 sort.64
  28.4 1.2 gather_fusion.3
  29.7 2.5 sort.62
  32.2 1.2 gather_fusion
  33.5 20.0 %all-gather.6.cloned.1.call-done = bf16[128,8192]{0,1:T(8,128)(2,1)} async-done(((bf16[128,1024]{0,1:T(8,128)(2,1)}), bf16[128,8192]{0,1:T(8,128)(2,1)}) %all-gather.6.cloned.1.call-update) | async-done | bytes 2097168 | tf_op jit(solution)/shard_map/all_gather | solution.py:49
  53.5 3.2 copy.59
  56.8 38.2 %all-gather.8.cloned.1.call-done = bf16[128,8192]{0,1:T(8,128)(2,1)} async-done(((bf16[128,1024]{0,1:T(8,128)(2,1)}), bf16[128,8192]{0,1:T(8,128)(2,1)}) %all-gather.8.cloned.1.call-update) | async-done | bytes 2097168 | tf_op jit(solution)/shard_map/all_gather | solution.py:69
  95.0 4.1 copy.66
  99.1 3.0 gather_fusion.4
  102.1 4.6 %gather_fusion.5 = bf16[128,128,128]{2,1,0:T(8,128)(2,1)} fusion(bf16[128,64,128]{2,0,1:T(8,128)(2,1)} %copy.66, s32[1024]{0:T(1024)S(1)} %pad_clamp_fusion.2), kind=kCustom, calls=%fused_computation.5 | custom fusion | bytes 8389120 | tf_op jit(solution)/shard_map/gather | solution.py:20
  106.8 5.2 %gather_fusion.1 = bf16[128,128,128]{2,1,0:T(8,128)(2,1)} fusion(bf16[128,128,128]{2,1,0:T(8,128)(2,1)} %bitcast.4, s32[1024]{0:T(1024)S(1)} %pad_clamp_fusion.5), kind=kCustom, calls=%fused_computation.1 | custom fusion | bytes 8389120 | tf_op jit(solution)/shard_map/gather | solution.py:36
  112.0 27.4 %all-gather.4.cloned.1.call-done = bf16[128,128,128]{2,1,0:T(8,128)(2,1)} async-done(((bf16[8,128,128]{2,1,0:T(8,128)(2,1)}), bf16[128,128,128]{2,1,0:T(8,128)(2,1)}) %all-gather.4.cloned.1.call-update) | async-done | bytes 4194320 | tf_op jit(solution)/shard_map/all_gather | solution.py:51
  139.4 5.2 %gather_fusion.2 = bf16[128,128,128]{2,1,0:T(8,128)(2,1)} fusion(bf16[128,128,128]{2,1,0:T(8,128)(2,1)} %all-gather.4.cloned.1.call-done, s32[1024]{0:T(1024)S(1)} %pad_clamp_fusion.4), kind=kCustom, calls=%fused_computation.2 | custom fusion | bytes 8389120 | tf_op jit(solution)/shard_map/gather | solution.py:36
  144.6 4.9 %convolution_bitcast_fusion.1 = f32[128,16,128]{0,2,1:T(8,128)S(1)} fusion(bf16[16,8,128,128]{3,2,1,0:T(8,128)(2,1)} %bitcast.77, bf16[128,16,8,128]{3,0,2,1:T(8,128)(2,1)} %bitcast.79), kind=kOutput, calls=%fused_computation.14 | convolution fusion | flops 536870912 | bytes 9437184 | tf_op jit(solution)/shard_map/thkb,hkbc->thc/dot_general | solution.py:53
  149.6 1.0 copy-done.5
  150.6 1.3 fusion.2
  151.9 0.8 copy-done.3
  152.7 3.3 convolution_convert_fusion.1
  156.1 5.2 %gather_fusion.6 = bf16[128,128,128]{2,1,0:T(8,128)(2,1)} fusion(bf16[128,128,128]{2,1,0:T(8,128)(2,1)} %bitcast.89, s32[1024]{0:T(1024)S(1)} %pad_clamp_fusion.1), kind=kCustom, calls=%fused_computation.6 | custom fusion | bytes 8389120 | tf_op jit(solution)/shard_map/gather | solution.py:90
  161.5 2.5 sort.65
  164.1 5.6 %convolution_convert_fusion = bf16[16,8,128,128]{3,2,1,0:T(8,128)(2,1)} fusion(bf16[128,16,8,128]{3,0,2,1:T(8,128)(2,1)} %bitcast.87, f32[128,16,128]{0,2,1:T(8,128)S(1)} %convolution_bitcast_fusion.1), kind=kOutput, calls=%fused_computation.10 | convolution fusion | flops 540278784 | bytes 9437184 | tf_op jit(solution)/shard_map/thb,thkc->hkbc/dot_general | solution.py:85
  169.7 6.4 %copy.74 = bf16[128,128,128]{2,1,0:T(8,128)(2,1)} copy(bf16[128,128,128]{1,2,0:T(8,128)(2,1)} %bitcast.90) | data formatting | bytes 8388608 | tf_op jit(solution)/shard_map/reshape | solution.py:89
  176.1 5.3 %gather_fusion.7 = bf16[128,128,128]{2,1,0:T(8,128)(2,1)} fusion(bf16[128,128,128]{2,1,0:T(8,128)(2,1)} %copy.74, s32[1024]{0:T(1024)S(1)} %pad_clamp_fusion), kind=kCustom, calls=%fused_computation.7 | custom fusion | bytes 8389120 | tf_op jit(solution)/shard_map/gather | solution.py:91
  181.4 6.7 %fusion.13 = f32[16,8,128,128]{3,2,1,0:T(8,128)} fusion(bf16[16,8,128,128]{3,2,1,0:T(8,128)(2,1)} %bitcast.78, bf16[128,16,128,1]{0,2,3,1:T(8,128)(2,1)S(1)} %fusion.2), kind=kOutput, calls=%fused_computation.40 | convolution fusion | flops 536870912 | bytes 13107200 | tf_op jit(solution)/shard_map/thc,hkbc->thkb/dot_general | solution.py:75
  188.2 9.0 %copy.68 = f32[128,128,128]{2,0,1:T(8,128)} copy(f32[128,128,128]{0,2,1:T(8,128)} %bitcast.83) | data formatting | bytes 16777216 | tf_op jit(solution)/shard_map/reshape | solution.py:27
  197.2 2.5 broadcast.44.clone.1
  199.7 26.7 %scatter_fusion.1 = f32[128,64,128]{2,0,1:T(8,128)} fusion(f32[128,64,128]{2,0,1:T(8,128)} %broadcast.44.clone.1, s32[128]{0:T(128)S(1)} %fusion.9, f32[128,128,128]{2,1,0:T(8,128)} %bitcast.82), kind=kCustom, calls=%fused_computation.9 | custom fusion | flops 2097152 | bytes 25166336 | tf_op jit(solution)/shard_map/scatter-add | solution.py:29
  226.3 2.6 convert_element_type.45
  229.0 2.9 copy.69
  232.0 6.8 %fusion.11 = f32[16,8,128,128]{3,2,1,0:T(8,128)} fusion(bf16[16,8,128,128]{3,2,1,0:T(8,128)(2,1)} %bitcast.85, f32[128,16,128]{0,2,1:T(8,128)S(1)} %convolution_bitcast_fusion.1), kind=kOutput, calls=%fused_computation.39 | convolution fusion | flops 538181632 | bytes 13631488 | tf_op jit(solution)/shard_map/thb,hkbc->thkc/dot_general | solution.py:62
  238.8 9.0 %copy.63 = f32[128,128,128]{2,0,1:T(8,128)} copy(f32[128,128,128]{0,2,1:T(8,128)} %bitcast.84) | data formatting | bytes 16777216 | tf_op jit(solution)/shard_map/reshape | solution.py:27
  247.8 2.5 broadcast.44.clone
  250.3 26.9 %scatter_fusion = f32[128,64,128]{2,0,1:T(8,128)} fusion(f32[128,64,128]{2,0,1:T(8,128)} %broadcast.44.clone, s32[128]{0:T(128)S(1)} %fusion.8, f32[128,128,128]{2,1,0:T(8,128)} %bitcast.81), kind=kCustom, calls=%fused_computation.8 | custom fusion | flops 2097152 | bytes 25166336 | tf_op jit(solution)/shard_map/scatter-add | solution.py:29
  277.2 2.6 convert_element_type.42
  279.8 2.9 copy.64
  282.8 16.4 %reduce-scatter.11.cloned.1.call-done = bf16[8,128,128]{2,1,0:T(8,128)(2,1)} async-done(((bf16[128,128,128]{2,1,0:T(8,128)(2,1)}), bf16[8,128,128]{2,1,0:T(8,128)(2,1)}) %reduce-scatter.11.cloned.1.call-update) | async-done | bytes 262160 | tf_op jit(solution)/shard_map/reduce_scatter | solution.py:96
  299.2 42.2 %reduce-scatter.7.cloned.1.call-done = bf16[128,1024]{0,1:T(8,128)(2,1)} async-done(((bf16[128,8192]{0,1:T(8,128)(2,1)}), bf16[128,1024]{0,1:T(8,128)(2,1)}) %reduce-scatter.7.cloned.1.call-update) | async-done | bytes 262160 | tf_op jit(solution)/shard_map/reduce_scatter | solution.py:79
  341.3 1.8 copy.76
  343.1 41.7 %reduce-scatter.5.cloned.1.call-done = bf16[128,1024]{0,1:T(8,128)(2,1)} async-done(((bf16[128,8192]{0,1:T(8,128)(2,1)}), bf16[128,1024]{0,1:T(8,128)(2,1)}) %reduce-scatter.5.cloned.1.call-update) | async-done | bytes 262160 | tf_op jit(solution)/shard_map/reduce_scatter | solution.py:66
  384.8 1.8 copy.75
  386.6 46.0 %all-reduce.3.cloned.1.call-done = (bf16[8,128,128]{2,1,0:T(8,128)(2,1)}, bf16[8,128,128]{2,1,0:T(8,128)(2,1)}) async-done(((bf16[8,128,128]{2,1,0:T(8,128)(2,1)}, bf16[8,128,128]{2,1,0:T(8,128)(2,1)}), (bf16[8,128,128]{2,1,0:T(8,128)(2,1)}, bf16[8,128,128]{2,1,0:T(8,128)(2,1)})) %all-reduce.3.cloned.1.call-update) | async-done | bytes 524304 | tf_op jit(solution)/shard_map/psum | solution.py:101
  432.6 1.8 convert_element_type.48
  434.4 1.8 convert_element_type.51
  (48 shorter events, 1.4 us)
Async XLA Ops:
  7.2 21.2 %copy-start = (s32[128,1]{0,1:T(1,128)S(1)}, s32[128,1]{0,1:T(1,128)}, u32[]{:S(2)}) copy-start(s32[128,1]{0,1:T(1,128)} %param.12) | copy-start | bytes 1540
  7.2 46.4 %all-gather.6.cloned.1.call-start = ((), (), s32[]{:S(2)}) async-start(), calls=%async_computation.6 | async-start | bytes 2359296 | tf_op jit(solution)/shard_map/all_gather | solution.py:49
  9.0 86.0 %all-gather.8.cloned.1.call-start = ((), (), s32[]{:S(2)}) async-start(), calls=%async_computation.8 | async-start | bytes 2359296 | tf_op jit(solution)/shard_map/all_gather | solution.py:69
  10.9 128.5 %all-gather.4.cloned.1.call-start = ((), (), s32[]{:S(2)}) async-start(), calls=%async_computation.5 | async-start | bytes 4456448 | tf_op jit(solution)/shard_map/all_gather | solution.py:51
  15.6 7.7 %copy-start.6 = (s32[128,1]{0,1:T(1,128)S(1)}, s32[128,1]{0,1:T(1,128)}, u32[]{:S(2)}) copy-start(s32[128,1]{0,1:T(1,128)} %param.13) | copy-start | bytes 1540
  15.6 14.0 %copy-start.7 = (s32[128,1]{0,1:T(1,128)S(1)}, s32[128,1]{0,1:T(1,128)}, u32[]{:S(2)}) copy-start(s32[128,1]{0,1:T(1,128)} %param.14) | copy-start | bytes 1540
  15.6 16.6 %copy-start.2 = (s32[128,1]{0,1:T(1,128)S(1)}, s32[128,1]{0,1:T(1,128)}, u32[]{:S(2)}) copy-start(s32[128,1]{0,1:T(1,128)} %param.15) | copy-start | bytes 1540
  15.6 91.1 %all-to-all-start = ((bf16[16,8,128,128]{3,2,1,0:T(8,128)(2,1)}), bf16[16,8,128,128]{3,2,1,0:T(8,128)(2,1)}, u32[]{:S(2)}, u32[]{:S(2)}) async-start(bf16[16,8,128,128]{3,2,1,0:T(8,128)(2,1)} %stack.2), calls=%async_computation | async-start | bytes 8388608 | tf_op jit(solution)/shard_map/all_to_all | solution.py:59
  23.3 259.5 %reduce-scatter.9.cloned.1.call-start = ((), (), s32[]{:S(2)}) async-start(), calls=%async_computation.10 | async-start | bytes 4456448 | tf_op jit(solution)/shard_map/reduce_scatter | solution.py:93
  144.6 4.9 %copy-start.4 = (bf16[128,128,128]{2,1,0:T(8,128)(2,1)S(1)}, bf16[128,128,128]{2,1,0:T(8,128)(2,1)}, u32[]{:S(2)}) copy-start(bf16[128,128,128]{2,1,0:T(8,128)(2,1)} %gather_fusion.1) | copy-start | bytes 12582916
  144.6 5.9 %copy-start.5 = (bf16[128,128,128]{2,1,0:T(8,128)(2,1)S(1)}, bf16[128,128,128]{2,1,0:T(8,128)(2,1)}, u32[]{:S(2)}) copy-start(bf16[128,128,128]{2,1,0:T(8,128)(2,1)} %gather_fusion.5) | copy-start | bytes 12582916
  150.5 2.2 copy-start.3
  161.3 137.8 %reduce-scatter.11.cloned.1.call-start = ((), (), s32[]{:S(2)}) async-start(), calls=%async_computation.11 | async-start | bytes 4456448 | tf_op jit(solution)/shard_map/reduce_scatter | solution.py:96
  181.4 159.9 %reduce-scatter.7.cloned.1.call-start = ((), (), s32[]{:S(2)}) async-start(), calls=%async_computation.9 | async-start | bytes 2359296 | tf_op jit(solution)/shard_map/reduce_scatter | solution.py:79
  232.0 152.9 %reduce-scatter.5.cloned.1.call-start = ((), (), s32[]{:S(2)}) async-start(), calls=%async_computation.7 | async-start | bytes 2359296 | tf_op jit(solution)/shard_map/reduce_scatter | solution.py:66
  277.2 159.0 %copy-start.1 = (s32[128,1]{0,1:T(1,128)S(1)}, s32[128,1]{0,1:T(1,128)}, u32[]{:S(2)}) copy-start(s32[128,1]{0,1:T(1,128)} %param.12) | copy-start | bytes 1540
  282.7 149.9 %all-reduce.3.cloned.1.call-start = ((), (), s32[]{:S(2)}) async-start(), calls=%async_computation.12 | async-start | bytes 1048576 | tf_op jit(solution)/shard_map/psum | solution.py:101
Sparse Core Ops, SparseCore 0:
  10.4 43.1 all-gather.5
  55.9 39.0 all-gather.7
  96.9 42.5 all-gather.3
  161.4 66.6 reduce-scatter.8
  230.5 68.6 reduce-scatter.10
  301.5 39.7 reduce-scatter.6
  343.9 40.8 reduce-scatter.4
  387.4 45.1 all-reduce.2
